TPU v7x, 1024 devices: a whole 4x8x16 slice. The times are simulated.
1024 devices in a mesh: grp: 4 (over y_hi), fsdp: 64 (over x, z), tp: 4 (over y_lo, core).
Axes of the slice: x: 4, y: 8 (y_hi: 4, y_lo: 2; y = y_hi * 2 + y_lo), z: 16, core: 2. Of those that a mesh axis runs over, the one named last changes fastest.
Arguments:
- image_rows: bfloat16 [98304, 8192], P(('grp', 'fsdp'), 'tp'), may hold values from -6 to 6
- enc_gain: bfloat16 [8192], P('tp'), may hold values from 0.099609375 to 1.8984375
- key_value_w: bfloat16 [8192, 1024], P(('tp', 'fsdp')), may hold values from -0.0625 to 0.0625
- tiles: int32 [384], P('fsdp'), may hold values from 1 to 4
- queries: bfloat16 [65536, 4096], P(('grp', 'fsdp'), 'tp'), may hold values from -6 to 6
Outputs:
- attended: bfloat16 [65536, 4096], P(('grp', 'fsdp'), 'tp')
Inputs may be any that keep to these rules, and one draw needn't show every extreme that they name: Each sample has 1 to 4 tiles.
All inputs are finite; a program needn't handle non-finite values.
Results may differ from a plain program's by a relative error of at most 0.0077.
Values may be sent and summed in bfloat16 or wider, within the bound.
A program may use at most 32 MiB of HBM per device.

v0:
```python
import jax
import jax.numpy as jnp
from jax import lax
from jax.sharding import PartitionSpec as P

D = 8192
HD = 128
KVH = 4
QH = 32
TILE_TOK = 16
SAMP = 2
TXT_S = 128
CAP = 64


def into_slots(block, per_group):
    parts = block.reshape((3, per_group) + block.shape[1:])
    empty = jnp.zeros((1, per_group) + block.shape[1:], block.dtype)
    return jnp.concatenate([empty, parts], axis=0)


def fold_rows(rows, piece):
    return jnp.dot(rows, piece, preferred_element_type=jnp.float32)


def shards(image_rows, enc_gain, key_value_w, tiles, queries):
    group = lax.axis_index("grp")
    per_group = image_rows.shape[0] // 3
    width = key_value_w.shape[1]
    heads_kv = width // (2 * HD)
    rows = image_rows.astype(jnp.float32)
    squares = lax.psum(jnp.sum(rows * rows, axis=1, keepdims=True), "tp")
    normed = (rows * lax.rsqrt(squares / D + 1e-05) * enc_gain.astype(jnp.float32)).astype(
        jnp.bfloat16
    )
    received = lax.all_to_all(
        into_slots(normed, per_group), "grp", split_axis=0, concat_axis=0, tiled=True
    )
    mine = received[0]
    total = fold_rows(mine, lax.all_gather(key_value_w, "fsdp", axis=0, tiled=True))
    heads = lax.psum_scatter(
        total.reshape(per_group, heads_kv, 2 * HD), "tp", scatter_dimension=1, tiled=True
    )
    kv = heads.astype(jnp.bfloat16)
    local_kv = kv.shape[1]
    groups_q = QH // KVH
    kv = kv.reshape(SAMP, CAP, local_kv, 2 * HD)
    keys = kv[..., :HD]
    values = kv[..., HD:]
    query = queries.reshape(SAMP, TXT_S, local_kv, groups_q, HD)
    counts = lax.dynamic_slice_in_dim(tiles, jnp.maximum(group - 1, 0) * SAMP, SAMP) * TILE_TOK
    live = jnp.arange(CAP)[None, :] < counts[:, None]
    scores = jnp.einsum("sikgd,sjkd->skgij", query, keys, preferred_element_type=jnp.float32) * (
        1.0 / HD**0.5
    )
    scores = jnp.where(live[:, None, None, None, :], scores, -1e30)
    top = jnp.max(scores, axis=-1, keepdims=True)
    expo = jnp.exp(scores - top)
    weights = (expo / jnp.sum(expo, axis=-1, keepdims=True)).astype(jnp.bfloat16)
    out = jnp.einsum(
        "skgij,sjkd->sikgd", weights, values, preferred_element_type=jnp.float32
    ).astype(jnp.bfloat16)
    out = jnp.where(group > 0, out, jnp.zeros_like(out))
    return out.reshape(queries.shape[0], queries.shape[1])


def solution(mesh):
    return jax.shard_map(
        shards,
        mesh=mesh,
        in_specs=(
            P(("grp", "fsdp"), "tp"),
            P("tp"),
            P(("tp", "fsdp"), None),
            P("fsdp"),
            P(("grp", "fsdp"), "tp"),
        ),
        out_specs=P(("grp", "fsdp"), "tp"),
        check_vma=False,
    )
```

profile of v0, /device:TPU:1, one launch (start us, length us, event | category | flops | bytes accessed | tf_op | source)
XLA Modules:
  0.0 217.7 jit_solution(5616306766271429739)
XLA Ops:
  6.5 0.0 all-gather.2.cloned.1.call-start
  6.5 0.7 all-gather.2.cloned.1.call-update
  7.3 0.7 convert_element_type.21
  7.9 1.8 fusion
  9.7 19.2 %psum.7 = f32[384,1]{0,1:T(1,128)S(1)} all-reduce(f32[384,1]{0,1:T(1,128)S(1)} %broadcast_in_dim.16), channel_id=1, replica_groups=mesh['grp'=4,'fsdp'=64,'tp'=4] {'tp'}, use_global_device_ids=true, to_apply=%region_1.0 | all-reduce | flops 384 | bytes 3072 | tf_op jit(solution)/shard_map/psum | solution.py:32
  28.9 1.8 fusion.2
  30.8 1.6 concatenate.3
  32.4 3.6 %all-to-all-start = ((bf16[4,128,2048]{2,1,0:T(8,128)(2,1)}), bf16[4,128,2048]{2,1,0:T(8,128)(2,1)S(1)}, u32[]{:S(2)}, u32[]{:S(2)}) async-start(bf16[4,128,2048]{2,1,0:T(8,128)(2,1)} %concatenate.3), calls=%async_computation | async-start | bytes 4194304 | tf_op jit(solution)/shard_map/all_to_all | solution.py:36
  36.0 0.0 reduce-scatter.2.cloned.1.call-start
  36.1 129.2 %all-gather.2.cloned.1.call-done = bf16[2048,1024]{1,0:T(8,128)(2,1)} async-done(((bf16[32,1024]{1,0:T(8,128)(2,1)}), bf16[2048,1024]{1,0:T(8,128)(2,1)}) %all-gather.2.cloned.1.call-update) | async-done | bytes 4194320 | tf_op jit(solution)/shard_map/all_gather | solution.py:40
  165.3 6.5 %copy.8 = bf16[1024,2048]{1,0:T(8,128)(2,1)} copy(bf16[1024,2048]{0,1:T(8,128)(2,1)} %bitcast.49) | data formatting | bytes 8388608 | tf_op jit(solution)/shard_map/dot_general | solution.py:23
  171.8 0.0 copy-start
  171.8 0.0 all-to-all-done
  171.8 0.0 copy-start.1
  171.8 4.6 %fusion.8 = f32[128,4,256]{2,0,1:T(8,128)} fusion(bf16[4,256,2048]{2,1,0:T(8,128)(2,1)} %bitcast.47, bf16[4,128,2048]{2,1,0:T(8,128)(2,1)S(1)} %all-to-all-done), kind=kOutput, calls=%fused_computation.14 | convolution fusion | flops 536870912 | bytes 5242880 | tf_op jit(solution)/shard_map/dot_general | solution.py:23
  176.3 0.0 reduce-scatter.2.cloned.1.call-update
  176.4 0.0 copy-done
  176.4 0.1 copy.13
  176.5 0.0 copy-done.1
  176.5 0.1 dynamic-slice_multiply_fusion
  176.6 0.1 iota_compare_fusion
  176.7 31.3 %reduce-scatter.2.cloned.1.call-done = f32[128,1,256]{2,0,1:T(8,128)} async-done(((f32[128,4,256]{2,0,1:T(8,128)}), f32[128,1,256]{2,0,1:T(8,128)}) %reduce-scatter.2.cloned.1.call-update) | async-done | bytes 131088 | tf_op jit(solution)/shard_map/reduce_scatter | solution.py:41
  208.0 0.9 convert_element_type.23
  208.9 0.3 fusion.13
  209.2 0.1 fusion.10
  209.3 0.4 fusion.4
  209.7 0.3 copy.10
  210.0 0.9 copy.20
  (2 shorter events, 0.0 us)
Async XLA Ops:
  6.5 158.7 %all-gather.2.cloned.1.call-start = ((), (), s32[]{:S(2)}) async-start(), calls=%async_computation.2 | async-start | bytes 4259840 | tf_op jit(solution)/shard_map/all_gather | solution.py:40
  32.4 139.4 %all-to-all-start = ((bf16[4,128,2048]{2,1,0:T(8,128)(2,1)}), bf16[4,128,2048]{2,1,0:T(8,128)(2,1)S(1)}, u32[]{:S(2)}, u32[]{:S(2)}) async-start(bf16[4,128,2048]{2,1,0:T(8,128)(2,1)} %concatenate.3), calls=%async_computation | async-start | bytes 4194304 | tf_op jit(solution)/shard_map/all_to_all | solution.py:36
  36.0 172.0 %reduce-scatter.2.cloned.1.call-start = ((), (), s32[]{:S(2)}) async-start(), calls=%async_computation.3 | async-start | bytes 655360 | tf_op jit(solution)/shard_map/reduce_scatter | solution.py:41
  171.8 4.6 %copy-start = (bf16[256,1024]{1,0:T(8,128)(2,1)S(1)}, bf16[256,1024]{1,0:T(8,128)(2,1)}, u32[]{:S(2)}) copy-start(bf16[256,1024]{1,0:T(8,128)(2,1)} %param.9) | copy-start | bytes 1572868
  171.8 4.7 %copy-start.1 = (s32[6]{0:T(128)S(1)}, s32[6]{0:T(128)}, u32[]{:S(2)}) copy-start(s32[6]{0:T(128)} %param.8) | copy-start | bytes 76
Sparse Core Ops, SparseCore 0:
  11.5 153.7 all-gather.1
  176.5 31.4 reduce-scatter.1
where the time goes:
time: 218 us
  waiting for transfers between devices  161 us (74%)
  blocking collectives  19.2 us (9%)
  between operations  13.5 us (6%)
  local copies, waits for them, and re-layouts  9.46 us (4%)
  other arithmetic  5.5 us (3%)
  matrix products  5.21 us (2%)
  starting transfers between devices  3.65 us (2%)
    all_gather x1, waiting for transfers between devices, shards(): lax.all_gather(key_value_w, 'fsdp', axis=0, tiled=True)  129 us
    reduce_scatter x1, waiting for transfers between devices, shards(): lax.psum_scatter(total.reshape(per_group, heads_kv, 2 * HD), 'tp', scatte...  31.3 us
    psum x1, blocking collectives, shards(): squares = lax.psum(jnp.sum(rows * rows, axis=1, keepdims=True), 'tp')  19.2 us
    dot_general x1, local copies, waits for them, and re-layouts, fold_rows(): return jnp.dot(rows, piece, preferred_element_type=jnp.float32)  6.52 us
    dot_general x1, matrix products, fold_rows(): return jnp.dot(rows, piece, preferred_element_type=jnp.float32)  4.55 us
  transfers between devices with their start and end apart: 3, of which 2 were waited for; matrix products, arithmetic and copies ran while one was open for 6% of the time, Pallas kernels for 0%

commit v1 on v0

v1 whole, which is shorter than its diff:
```python
import jax
import jax.numpy as jnp
from jax import lax
from jax.experimental import pallas as pl
from jax.experimental.pallas import tpu as pltpu
from jax.sharding import PartitionSpec as P

D = 8192
HD = 128
KVH = 4
QH = 32
TILE_TOK = 16
SAMP = 2
TXT_S = 128
CAP = 64
IMG = 128
NX = 4
NZ = 16
HALF = NZ // 2
PIECE = 32
SPLIT = 384
MESH = pl.DeviceIdType.MESH


def project(
    rows_hbm, gain_ref, w_hbm, out_ref,
    rows, normed, wfull, mine, theirs, packed, stat,
    local_sem, stat_send, stat_recv,
    ax_send, ax_recv, az_send, az_recv, bz_send, bz_recv, bx_send, bx_recv, bf_send, bf_recv,
    core_send, core_recv, y_send, y_recv, ready,
):
    g = lax.axis_index("grp")
    f = lax.axis_index("fsdp")
    t = lax.axis_index("tp")
    x, z = f // NZ, f % NZ
    ylo, core = t // 2, t % 2

    def at(x1, z1):
        return (0, x1 * NZ + z1, t)

    def xs(step):
        return (x + step + NX) % NX

    def zs(step):
        return (z + step + NZ) % NZ

    barrier = pltpu.get_barrier_semaphore()

    @pl.when(g == 0)
    def _():
        own_w = pltpu.make_async_copy(w_hbm, wfull.at[x, z], local_sem.at[0])
        own_rows = pltpu.make_async_copy(rows_hbm, rows, local_sem.at[1])
        own_w.start()
        own_rows.start()
        for d in (1, -1):
            pl.semaphore_signal(barrier, inc=1, device_id=at(x, zs(d)), device_id_type=MESH)
        for d in (1, 2, 3):
            pl.semaphore_signal(barrier, inc=1, device_id=at(xs(d), z), device_id_type=MESH)
            pl.semaphore_signal(barrier, inc=1, device_id=(0, f, (t + d) % 4), device_id_type=MESH)
        for gg in (1, 2, 3):
            for yy in (0, 1):
                pl.semaphore_signal(barrier, inc=1, device_id=(gg, f, yy * 2 + core), device_id_type=MESH)
        own_w.wait()
        pl.semaphore_wait(barrier, 8)

        acols, bcols = pl.ds(0, SPLIT), pl.ds(SPLIT, 1024 - SPLIT)
        sends = []

        def push(src, dst, ssem, rsem, dev):
            c = pltpu.make_async_remote_copy(
                src_ref=src, dst_ref=dst, send_sem=ssem, recv_sem=rsem, device_id=dev, device_id_type=MESH
            )
            c.start()
            sends.append(c)
            return c

        def got(dst, rsem):
            pltpu.make_async_copy(dst, dst, rsem).wait()

        def zdir(d):
            return 1 if d == 0 else -1

        def send_a_z(step):
            for d in (0, 1):
                zz = zs(-zdir(d) * step)
                half = pl.ds(2 * d, 2) if step == HALF - 1 else pl.ds(0, NX)
                ref = wfull.at[half, zz, :, acols]
                push(ref, ref, az_send.at[d, step], az_recv.at[d, step], at(x, zs(zdir(d))))

        def got_a_z(step):
            for d in (0, 1):
                zz = zs(-zdir(d) * (step + 1))
                half = pl.ds(2 * d, 2) if step == HALF - 1 else pl.ds(0, NX)
                got(wfull.at[half, zz, :, acols], az_recv.at[d, step])

        def rows_b(d, last):
            return pl.ds(16 * d, 16) if last else pl.ds(0, PIECE)

        def send_b_z(step):
            for d in (0, 1):
                zz = zs(-zdir(d) * step)
                ref = wfull.at[x, zz, rows_b(d, step == HALF - 1), bcols]
                push(ref, ref, bz_send.at[d, step], bz_recv.at[d, step], at(x, zs(zdir(d))))

        def got_b_z(step):
            for d in (0, 1):
                zz = zs(-zdir(d) * (step + 1))
                got(wfull.at[x, zz, rows_b(d, step == HALF - 1), bcols], bz_recv.at[d, step])

        def held(step):
            if step == 0:
                return [(0, z)]
            if step == HALF:
                return [(0, zs(HALF))]
            return [(0, zs(-step)), (1, zs(step))]

        def send_b_x(step):
            for k, zz in held(step):
                for d in (0, 1):
                    ref = wfull.at[x, zz, :, bcols]
                    push(ref, ref, bx_send.at[d, k, step], bx_recv.at[d, k, step], at(xs(zdir(d)), z))

        def relay_b_x(step):
            for k, zz in held(step):
                for d in (0, 1):
                    xx = xs(-zdir(d))
                    got(wfull.at[xx, zz, :, bcols], bx_recv.at[d, k, step])
                    ref = wfull.at[xx, zz, pl.ds(16 * d, 16), bcols]
                    push(ref, ref, bf_send.at[d, k, step], bf_recv.at[d, k, step], at(xs(zdir(d)), z))

        def got_b_f(step):
            for k, zz in held(step):
                for d in (0, 1):
                    got(wfull.at[xs(2), zz, pl.ds(16 * d, 16), bcols], bf_recv.at[d, k, step])

        own_a = wfull.at[x, z, :, acols]
        send_b_z(0)
        for d in (1, 2, 3):
            push(own_a, own_a, ax_send.at[d - 1], ax_recv.at[d - 1], at(xs(d), z))
        send_b_x(0)

        own_rows.wait()
        total = jnp.zeros((3 * IMG, 128), jnp.float32)
        for j in range(NZ):
            part = rows[:, j * 128:(j + 1) * 128].astype(jnp.float32)
            total = total + part * part
        line = jnp.sum(jnp.transpose(total), axis=0, keepdims=True)
        stat[0] = jnp.broadcast_to(line, (8, 3 * IMG))
        for d in (1, 2, 3):
            push(stat.at[0], stat.at[d], stat_send.at[d - 1], stat_recv.at[d - 1], (0, f, (t + d) % 4))
        for d in (1, 2, 3):
            got(wfull.at[xs(-d), z, :, acols], ax_recv.at[d - 1])
        send_a_z(0)

        def normalise():
            for d in (1, 2, 3):
                got(stat.at[d], stat_recv.at[d - 1])
            squares = (stat[0] + stat[1]) + (stat[2] + stat[3])
            inv = lax.rsqrt(squares[0:1] / D + 1e-05)
            column = jnp.transpose(jnp.broadcast_to(inv, (128, 3 * IMG)))
            for j in range(NZ):
                cols = slice(j * 128, (j + 1) * 128)
                normed[:, cols] = (
                    rows[:, cols].astype(jnp.float32) * column * gain_ref[:, cols].astype(jnp.float32)
                ).astype(jnp.bfloat16)

        for step in range(HALF):
            got_b_z(step)
            if step < HALF - 1:
                send_b_z(step + 1)
            send_b_x(step + 1)
            got_a_z(step)
            if step < HALF - 1:
                send_a_z(step + 1)
            relay_b_x(step)
            if step == 1:
                normalise()
        relay_b_x(HALF)
        for step in range(HALF + 1):
            got_b_f(step)

        def head(h):
            cols = pl.ds(pl.multiple_of(h * 256, 256), 256)
            w = wfull[:, :, :, cols].reshape(NX * NZ * PIECE, 256)
            return jnp.dot(normed[...], w, preferred_element_type=jnp.float32)

        sibling = (0, f, ylo * 2 + 1 - core)
        for k in (0, 1):
            mine[k] = head(2 * k + 1 - core)
            push(mine.at[k], theirs.at[k], core_send.at[k], core_recv.at[k], sibling)
        pl.semaphore_wait(ready, 6)
        for k in (0, 1):
            own = head(2 * k + core)
            got(theirs.at[k], core_recv.at[k])
            packed[k] = (own + theirs[k]).astype(jnp.bfloat16)
            for gg in (1, 2, 3):
                push(
                    packed.at[k, pl.ds((gg - 1) * IMG, IMG)], out_ref.at[ylo],
                    y_send.at[gg - 1, k], y_recv.at[ylo], (gg, f, k * 2 + core),
                )
        for c in sends:
            c.wait_send()

    @pl.when(g > 0)
    def _():
        pl.semaphore_wait(barrier, 2)
        for yy in (0, 1):
            pl.semaphore_signal(ready, inc=1, device_id=(0, f, yy * 2 + core), device_id_type=MESH)
        for yy in (0, 1):
            pltpu.make_async_copy(out_ref.at[yy], out_ref.at[yy], y_recv.at[yy]).wait()


def attend(tiles_ref, part_ref, q_ref, o_ref):
    g = lax.axis_index("grp")

    @pl.when(g == 0)
    def _():
        o_ref[...] = jnp.zeros_like(o_ref)

    @pl.when(g > 0)
    def _():
        kv = (part_ref[0].astype(jnp.float32) + part_ref[1].astype(jnp.float32)).astype(jnp.bfloat16)
        slot = lax.broadcasted_iota(jnp.int32, (TXT_S, CAP), 1)
        for s in range(SAMP):
            keys = kv[s * CAP:(s + 1) * CAP, :HD]
            values = kv[s * CAP:(s + 1) * CAP, HD:]
            live = slot < tiles_ref[(g - 1) * SAMP + s] * TILE_TOK
            for h in range(QH // KVH):
                q = q_ref[s * TXT_S:(s + 1) * TXT_S, h * HD:(h + 1) * HD]
                scores = lax.dot_general(
                    q, keys, (((1,), (1,)), ((), ())), preferred_element_type=jnp.float32
                ) * (1.0 / HD**0.5)
                scores = jnp.where(live, scores, -1e30)
                expo = jnp.exp(scores - jnp.max(scores, axis=-1, keepdims=True))
                weights = (expo / jnp.sum(expo, axis=-1, keepdims=True)).astype(jnp.bfloat16)
                o_ref[s * TXT_S:(s + 1) * TXT_S, h * HD:(h + 1) * HD] = jnp.dot(
                    weights, values, preferred_element_type=jnp.float32
                ).astype(jnp.bfloat16)


def shards(image_rows, enc_gain, key_value_w, tiles, queries):
    dma = pltpu.SemaphoreType.DMA
    anywhere = pl.BlockSpec(memory_space=pl.ANY)
    vmem = pl.BlockSpec(memory_space=pltpu.VMEM)
    parts = pl.pallas_call(
        project,
        out_shape=jax.ShapeDtypeStruct((2, IMG, 2 * HD), jnp.bfloat16),
        in_specs=[anywhere, vmem, anywhere],
        out_specs=anywhere,
        scratch_shapes=[
            pltpu.VMEM((3 * IMG, 2048), jnp.bfloat16),
            pltpu.VMEM((3 * IMG, 2048), jnp.bfloat16),
            pltpu.VMEM((NX, NZ, PIECE, 1024), jnp.bfloat16),
            pltpu.VMEM((2, 3 * IMG, 256), jnp.float32),
            pltpu.VMEM((2, 3 * IMG, 256), jnp.float32),
            pltpu.VMEM((2, 3 * IMG, 256), jnp.bfloat16),
            pltpu.VMEM((4, 8, 3 * IMG), jnp.float32),
            dma((2,)),
            dma((3,)),
            dma((3,)),
            dma((3,)),
            dma((3,)),
            dma((2, HALF)),
            dma((2, HALF)),
            dma((2, HALF)),
            dma((2, HALF)),
            dma((2, 2, HALF + 1)),
            dma((2, 2, HALF + 1)),
            dma((2, 2, HALF + 1)),
            dma((2, 2, HALF + 1)),
            dma((2,)),
            dma((2,)),
            dma((3, 2)),
            dma((2,)),
            pltpu.SemaphoreType.REGULAR,
        ],
        compiler_params=pltpu.CompilerParams(
            collective_id=0, has_side_effects=True, vmem_limit_bytes=32 << 20
        ),
        name="project",
    )(image_rows, enc_gain.reshape(1, -1), key_value_w)
    return pl.pallas_call(
        attend,
        out_shape=jax.ShapeDtypeStruct(queries.shape, jnp.bfloat16),
        in_specs=[pl.BlockSpec(memory_space=pltpu.SMEM), vmem, vmem],
        out_specs=vmem,
        compiler_params=pltpu.CompilerParams(vmem_limit_bytes=16 << 20),
        name="attend",
    )(tiles, parts, queries)


def solution(mesh):
    return jax.shard_map(
        shards,
        mesh=mesh,
        in_specs=(
            P(("grp", "fsdp"), "tp"),
            P("tp"),
            P(("tp", "fsdp"), None),
            P("fsdp"),
            P(("grp", "fsdp"), "tp"),
        ),
        out_specs=P(("grp", "fsdp"), "tp"),
        check_vma=False,
    )
```

time: 218 us -> 83.2 us (0.38)
  waiting for transfers between devices: 161 us -> 0 us
  Pallas kernels: 0 us -> 78.9 us
  blocking collectives: 19.2 us -> 0 us
  between operations: 13.5 us -> 0.03 us
  local copies, waits for them, and re-layouts: 9.46 us -> 2.96 us
  other arithmetic: 5.5 us -> 0 us
  matrix products: 5.21 us -> 0 us
  starting transfers between devices: 3.65 us -> 0 us
    all_gather x1 -> x0, waiting for transfers between devices: 129 us -> none  [shards(): lax.all_gather(key_value_w, 'fsdp', axis=0, tiled=True)]
    pallas_call x0 -> x2, Pallas kernels: none -> 78.9 us  [the longest x1 77.5 us: shards(): pl.pallas_call(project, out_shape=jax.ShapeDtypeStruct((2, IMG, 2 * HD),...]
    reduce_scatter x1 -> x0, waiting for transfers between devices: 31.3 us -> none  [shards(): lax.psum_scatter(total.reshape(per_group, heads_kv, 2 * HD), 'tp', scatte...]
    psum x1 -> x0, blocking collectives: 19.2 us -> none  [shards(): squares = lax.psum(jnp.sum(rows * rows, axis=1, keepdims=True), 'tp')]
    dot_general x1 -> x0, local copies, waits for them, and re-layouts: 6.52 us -> none  [fold_rows(): return jnp.dot(rows, piece, preferred_element_type=jnp.float32)]
    dot_general x3 -> x0, matrix products: 5.21 us -> none  [the longest x1 4.55 us: fold_rows(): return jnp.dot(rows, piece, preferred_element_type=jnp.float32)]
    all_to_all x1 -> x0, starting transfers between devices: 3.61 us -> none  [shards(): lax.all_to_all(into_slots(normed, per_group), 'grp', split_axis=0, concat...]
    convert_element_type x3 -> x0, other arithmetic: 3.43 us -> none  [the longest x1 1.83 us: shards(): (rows * lax.rsqrt(squares / D + 1e-05) * enc_gain.astype(jnp.float32)).as...]
  transfers between devices with their start and end apart: 3 -> 0, of which waited for: 2 -> 0; matrix products, arithmetic and copies ran while one was open for 6% -> 0% of each run, Pallas kernels for 0% -> 0%
where the time goes in v1:
time: 83.2 us; the launch traced here: 81.9 us
  Pallas kernels  78.9 us (95%)
  local copies, waits for them, and re-layouts  2.96 us (4%)
    pallas_call x1, Pallas kernels, shards(): pl.pallas_call(project, out_shape=jax.ShapeDtypeStruct((2, IMG, 2 * HD),...  77.5 us
    unnamed x8, local copies, waits for them, and re-layouts  2.25 us

profile of v1, /device:TPU:1, one launch (start us, length us, event | category | flops | bytes accessed | tf_op | source)
XLA Modules:
  0.0 81.9 jit_solution(17932497234675144372)
XLA Ops:
  0.0 0.0 copy-start.3
  0.0 0.7 reshape.3.gain_ref
  0.7 0.0 copy-start
  0.7 1.4 %copy-done = bf16[384,2048]{1,0:T(8,128)(2,1)S(1)} copy-done((bf16[384,2048]{1,0:T(8,128)(2,1)S(1)}, bf16[384,2048]{1,0:T(8,128)(2,1)}, u32[]{:S(2)}) %copy-start) | copy-done | bytes 1572888
  2.1 0.0 copy-start.2
  2.1 0.8 %copy-done.2 = bf16[32,1024]{1,0:T(8,128)(2,1)S(1)} copy-done((bf16[32,1024]{1,0:T(8,128)(2,1)S(1)}, bf16[32,1024]{1,0:T(8,128)(2,1)}, u32[]{:S(2)}) %copy-start.2) | copy-done | bytes 65560
  3.0 0.0 copy-start.1
  3.0 77.5 %project.1.part_ref = bf16[2,128,256]{2,1,0:T(8,128)(2,1)S(1)} custom-call(bf16[384,2048]{1,0:T(8,128)(2,1)S(1)} %copy-done, bf16[1,2048]{1,0:T(2,128)(2,1)S(1)} %reshape.3.gain_ref, bf16[32,1024]{1,0:T(8,128)(2,1)S(1)} %copy-done.2), custom_call_target="tpu_custom_call" | custom-call | tf_op jit(solution)/shard_map/project/pallas_call | solution.py:245
  80.5 0.0 copy-done.3
  80.5 0.0 copy-done.1
  80.5 1.4 %attend.1 = bf16[256,1024]{1,0:T(8,128)(2,1)} custom-call(s32[6]{0:T(128)S(1)} %copy-done.3, bf16[2,128,256]{2,1,0:T(8,128)(2,1)S(1)} %project.1.part_ref, bf16[256,1024]{1,0:T(8,128)(2,1)S(1)} %copy-done.1), custom_call_target="tpu_custom_call" | custom-call | tf_op jit(solution)/shard_map/attend/pallas_call | solution.py:282
Async XLA Ops:
  0.0 80.5 %copy-start.3 = (s32[6]{0:T(128)S(1)}, s32[6]{0:T(128)}, u32[]{:S(2)}) copy-start(s32[6]{0:T(128)} %tiles_ref.1) | copy-start | bytes 76
  0.7 1.4 %copy-start = (bf16[384,2048]{1,0:T(8,128)(2,1)S(1)}, bf16[384,2048]{1,0:T(8,128)(2,1)}, u32[]{:S(2)}) copy-start(bf16[384,2048]{1,0:T(8,128)(2,1)} %rows_hbm.1) | copy-start | bytes 4718596
  2.1 0.8 %copy-start.2 = (bf16[32,1024]{1,0:T(8,128)(2,1)S(1)}, bf16[32,1024]{1,0:T(8,128)(2,1)}, u32[]{:S(2)}) copy-start(bf16[32,1024]{1,0:T(8,128)(2,1)} %w_hbm.1) | copy-start | bytes 196612
  3.0 77.5 %copy-start.1 = (bf16[256,1024]{1,0:T(8,128)(2,1)S(1)}, bf16[256,1024]{1,0:T(8,128)(2,1)}, u32[]{:S(2)}) copy-start(bf16[256,1024]{1,0:T(8,128)(2,1)} %q_ref.1) | copy-start | bytes 1572868

commit v2 on v0

v2 whole, which is shorter than its diff:
```python
import jax
import jax.numpy as jnp
from jax import lax
from jax.experimental import pallas as pl
from jax.experimental.pallas import tpu as pltpu
from jax.sharding import PartitionSpec as P

D = 8192
HD = 128
KVH = 4
QH = 32
TILE_TOK = 16
SAMP = 2
TXT_S = 128
CAP = 64
IMG = 128
NX = 4
NZ = 16
FAR = 6
PIECE = 32
PART = 512
SPARE = 2
MESH = pl.DeviceIdType.MESH


def project(
    rows_hbm, gain_hbm, w_hbm, out_ref,
    rows, gain_ref, inbox, normed, wz, mine, theirs, packed, stat, scale, scale_in,
    local_sem, rows_send, rows_recv, stat_send, stat_recv, scale_send, scale_recv,
    far_send, far_recv, near_send, near_recv, core_send, core_recv, part_send, part_recv, ready,
):
    g = lax.axis_index("grp")
    f = lax.axis_index("fsdp")
    t = lax.axis_index("tp")
    x, z = f // NZ, f % NZ
    ylo, core = t // 2, t % 2

    def xs(step):
        return (x + step + NX) % NX

    def zs(step):
        return (z + step + NZ) % NZ

    def chip(gg, x1, z1, t1):
        return (gg, x1 * NZ + z1, t1)

    barrier = pltpu.get_barrier_semaphore()

    def hello(dev):
        pl.semaphore_signal(barrier, inc=1, device_id=dev, device_id_type=MESH)

    def copy(src, dst, ssem, rsem, dev):
        return pltpu.make_async_remote_copy(
            src_ref=src, dst_ref=dst, send_sem=ssem, recv_sem=rsem, device_id=dev, device_id_type=MESH
        )

    def got(dst, rsem):
        pltpu.make_async_copy(dst, dst, rsem).wait()

    def way(d):
        return 1 if d == 0 else -1

    @pl.when(g == SPARE)
    def _():
        pl.semaphore_wait(barrier, 8)

    @pl.when(g != SPARE)
    def _():
        own_w = pltpu.make_async_copy(w_hbm, wz.at[z], local_sem.at[0])
        own_gain = pltpu.make_async_copy(gain_hbm, gain_ref, local_sem.at[1])
        own_rows = pltpu.make_async_copy(rows_hbm, rows, local_sem.at[2])
        own_w.start()
        own_gain.start()
        for d in (1, -1, FAR, -FAR):
            hello(chip(g, x, zs(d), t))

        @pl.when(g == 0)
        def _():
            own_rows.start()
            for d in (1, 2, 3):
                hello((0, f, (t + d) % 4))
                hello(chip(0, xs(d), z, t))
            for gg in (1, 3):
                for xd in range(NX):
                    hello(chip(gg, xs(xd), z, t))
            for xd in range(NX):
                for yy in (0, 1):
                    hello(chip(SPARE, xs(xd), z, yy * 2 + core))

        @pl.when(g > 0)
        def _():
            for xd in range(NX):
                hello(chip(0, xs(xd), z, t))
                hello(chip(g, xs(xd), z, (1 - ylo) * 2 + core))
            for xd in (1, 2, 3):
                hello(chip(g, xs(xd), z, t))
            hello((g, f, ylo * 2 + 1 - core))

        own_w.wait()
        own_gain.wait()

        @pl.when(g == 0)
        def _():
            pl.semaphore_wait(barrier, 18)

        @pl.when(g > 0)
        def _():
            pl.semaphore_wait(barrier, 16)

        sends = []

        def push(*a):
            c = copy(*a)
            c.start()
            sends.append(c)

        def cols(c):
            return pl.ds(c * PART, PART)

        def moved(o, d):
            return o - way(d)

        def cut(o, d):
            return pl.ds(16 * d, 16) if abs(o) == NZ // 2 else pl.ds(0, PIECE)

        def near(o, d, c):
            m = moved(o, d)
            ref = wz.at[zs(o), cut(m, d), cols(c)]
            push(ref, ref, near_send.at[d, c, m % NZ], near_recv.at[d, c, m % NZ], chip(g, x, zs(way(d)), t))

        def got_near(o, d, c):
            got(wz.at[zs(o), cut(o, d), cols(c)], near_recv.at[d, c, o % NZ])

        for c in (0, 1):
            for d in (0, 1):
                ref = wz.at[z, :, cols(c)]
                push(ref, ref, far_send.at[d, c], far_recv.at[d, c], chip(g, x, zs(FAR * way(d)), t))

        def rows_copy(i, gg, block, xd):
            src = rows_hbm.at[pl.ds(block * IMG, IMG), pl.ds(pl.multiple_of(xs(xd) * PART, PART), PART)]
            return copy(src, inbox.at[x], rows_send.at[i, xd], rows_recv.at[x], chip(gg, xs(xd), z, t))

        targets = ((1, 0), (3, 2), (0, 1))

        def own_inbox():
            src = rows_hbm.at[pl.ds(IMG, IMG), pl.ds(pl.multiple_of(x * PART, PART), PART)]
            return pltpu.make_async_copy(src, inbox.at[x], rows_recv.at[x])

        @pl.when(g == 0)
        def _():
            for xd in range(NX):
                for i, (gg, block) in enumerate(targets):
                    if gg == 0 and xd == 0:
                        own_inbox().start()
                    else:
                        rows_copy(i, gg, block, xd).start()

        for c in (0, 1):
            for d in (0, 1):
                near(0, d, c)

        def stat_copy(d):
            return copy(stat.at[0], stat.at[d], stat_send.at[d - 1], stat_recv.at[d - 1], (0, f, (t + d) % 4))

        @pl.when(g == 0)
        def _():
            own_rows.wait()
            total = jnp.zeros((3 * IMG, 128), jnp.float32)
            for j in range(NZ):
                part = rows[:, j * 128:(j + 1) * 128].astype(jnp.float32)
                total = total + part * part
            line = jnp.sum(jnp.transpose(total), axis=0, keepdims=True)
            stat[0] = jnp.broadcast_to(line, (8, 3 * IMG))
            for d in (1, 2, 3):
                stat_copy(d).start()

        for c in (0, 1):
            for d in (0, 1):
                got_near(-way(d), d, c)
                near(-way(d), d, c)

        def scale_copy(i, gg, block, xd):
            return copy(
                scale.at[block], scale_in.at[x], scale_send.at[i, xd], scale_recv.at[x], chip(gg, xs(xd), z, t)
            )

        @pl.when(g == 0)
        def _():
            for d in (1, 2, 3):
                got(stat.at[d], stat_recv.at[d - 1])
            both = (stat[0] + stat[1]) + (stat[2] + stat[3])
            inv = lax.rsqrt(both / D + 1e-05)
            for block in range(3):
                scale[block] = inv[:, block * IMG:(block + 1) * IMG]
            for xd in range(NX):
                for i, (gg, block) in enumerate(targets):
                    if gg == 0 and xd == 0:
                        pltpu.make_async_copy(scale.at[block], scale_in.at[x], scale_recv.at[x]).start()
                    else:
                        scale_copy(i, gg, block, xd).start()

        for c in (0, 1):
            for d in (0, 1):
                got_near(-2 * way(d), d, c)
                near(-2 * way(d), d, c)
        for c in (0, 1):
            for d in (0, 1):
                got(wz.at[zs(-FAR * way(d)), :, cols(c)], far_recv.at[d, c])
            for d in (0, 1):
                near(-FAR * way(d), d, c)
                near(FAR * way(d), d, c)
        for c in (0, 1):
            for d in (0, 1):
                got_near(-7 * way(d), d, c)
                near(-7 * way(d), d, c)
                got_near(5 * way(d), d, c)
                near(5 * way(d), d, c)

        gains = []
        for j in range(PART // 128):
            pick = gain_ref[j * 128:(j + 1) * 128]
            for i in (1, 2, 3):
                pick = jnp.where(x == i, gain_ref[i * PART + j * 128:i * PART + (j + 1) * 128], pick)
            gains.append(pick.astype(jnp.float32).reshape(1, 128))
        for i in range(NX):
            got(inbox.at[i], rows_recv.at[i])
            got(scale_in.at[i], scale_recv.at[i])
            column = jnp.transpose(jnp.broadcast_to(scale_in[i, 0:1], (128, IMG)))
            for j in range(PART // 128):
                lanes = slice(j * 128, (j + 1) * 128)
                normed[i * IMG:(i + 1) * IMG, lanes] = (
                    inbox[i, :, lanes].astype(jnp.float32) * column * gains[j]
                ).astype(jnp.bfloat16)

        for c in (0, 1):
            for d in (0, 1):
                got_near(-3 * way(d), d, c)
                got_near(-8 * way(d), d, c)
                got_near(4 * way(d), d, c)

        def head(h):
            w = wz[:, :, pl.ds(pl.multiple_of(h * 256, 256), 256)].reshape(PART, 256)
            return jnp.dot(normed[...], w, preferred_element_type=jnp.float32)

        def side(j):
            return ylo if j == 0 else 1 - ylo

        order = (1, 0)
        for j in order:
            mine[j] = head(side(j) * 2 + 1 - core)
            push(mine.at[j], theirs.at[j], core_send.at[j], core_recv.at[j], (g, f, ylo * 2 + 1 - core))

        home = jnp.where(g == 0, SPARE, g)
        slot = x * 2 + ylo

        @pl.when(g == 0)
        def _():
            pl.semaphore_wait(ready, 8)

        def own_part():
            return copy(
                packed.at[0, pl.ds(pl.multiple_of(x * IMG, IMG), IMG)], out_ref.at[slot],
                part_send.at[0, 0], part_recv.at[slot], chip(SPARE, x, z, t),
            )

        for j in order:
            own = head(side(j) * 2 + core)
            got(theirs.at[j], core_recv.at[j])
            packed[j] = (own + theirs[j]).astype(jnp.bfloat16)
            for xd in (2, 1, 3, 0):
                src = packed.at[j, pl.ds(pl.multiple_of(xs(xd) * IMG, IMG), IMG)]
                if j == 0 and xd == 0:
                    @pl.when(g == 0)
                    def _():
                        own_part().start()

                    @pl.when(g > 0)
                    def _():
                        pltpu.make_async_copy(src, out_ref.at[slot], part_recv.at[slot]).start()
                else:
                    push(
                        src, out_ref.at[slot], part_send.at[j, xd], part_recv.at[slot],
                        chip(home, xs(xd), z, side(j) * 2 + core),
                    )

        @pl.when(g == 0)
        def _():
            own_part().wait_send()
            for d in (1, 2, 3):
                stat_copy(d).wait_send()
            for xd in range(NX):
                for i, (gg, block) in enumerate(targets):
                    if gg != 0 or xd != 0:
                        rows_copy(i, gg, block, xd).wait_send()
                        scale_copy(i, gg, block, xd).wait_send()

        for c in sends:
            c.wait_send()

    @pl.when(g == SPARE)
    def _():
        for xd in range(NX):
            for yy in (0, 1):
                pl.semaphore_signal(
                    ready, inc=1, device_id=chip(0, xs(xd), z, yy * 2 + core), device_id_type=MESH
                )

    @pl.when(g > 0)
    def _():
        for i in range(2 * NX):
            got(out_ref.at[i], part_recv.at[i])


def attend(tiles_ref, part_ref, q_ref, o_ref):
    g = lax.axis_index("grp")

    @pl.when(g == 0)
    def _():
        o_ref[...] = jnp.zeros_like(o_ref)

    @pl.when(g > 0)
    def _():
        kv = part_ref[0].astype(jnp.float32)
        for i in range(1, 2 * NX):
            kv = kv + part_ref[i].astype(jnp.float32)
        kv = kv.astype(jnp.bfloat16)
        slot = lax.broadcasted_iota(jnp.int32, (TXT_S, CAP), 1)
        for s in range(SAMP):
            keys = kv[s * CAP:(s + 1) * CAP, :HD]
            values = kv[s * CAP:(s + 1) * CAP, HD:]
            live = slot < tiles_ref[(g - 1) * SAMP + s] * TILE_TOK
            for h in range(QH // KVH):
                q = q_ref[s * TXT_S:(s + 1) * TXT_S, h * HD:(h + 1) * HD]
                scores = lax.dot_general(
                    q, keys, (((1,), (1,)), ((), ())), preferred_element_type=jnp.float32
                ) * (1.0 / HD**0.5)
                scores = jnp.where(live, scores, -1e30)
                expo = jnp.exp(scores - jnp.max(scores, axis=-1, keepdims=True))
                weights = (expo / jnp.sum(expo, axis=-1, keepdims=True)).astype(jnp.bfloat16)
                o_ref[s * TXT_S:(s + 1) * TXT_S, h * HD:(h + 1) * HD] = jnp.dot(
                    weights, values, preferred_element_type=jnp.float32
                ).astype(jnp.bfloat16)


def shards(image_rows, enc_gain, key_value_w, tiles, queries):
    dma = pltpu.SemaphoreType.DMA
    bf16, f32 = jnp.bfloat16, jnp.float32
    hbm = pl.BlockSpec(memory_space=pltpu.HBM)
    vmem = pl.BlockSpec(memory_space=pltpu.VMEM)
    parts = pl.pallas_call(
        project,
        out_shape=jax.ShapeDtypeStruct((2 * NX, IMG, 2 * HD), bf16),
        in_specs=[hbm, hbm, hbm],
        out_specs=hbm,
        scratch_shapes=[
            pltpu.VMEM((3 * IMG, 2048), bf16),
            pltpu.VMEM((2048,), bf16),
            pltpu.VMEM((NX, IMG, PART), bf16),
            pltpu.VMEM((NX * IMG, PART), bf16),
            pltpu.VMEM((NZ, PIECE, 1024), bf16),
            pltpu.VMEM((2, NX * IMG, 256), f32),
            pltpu.VMEM((2, NX * IMG, 256), f32),
            pltpu.VMEM((2, NX * IMG, 256), bf16),
            pltpu.VMEM((4, 8, 3 * IMG), f32),
            pltpu.VMEM((3, 8, IMG), f32),
            pltpu.VMEM((NX, 8, IMG), f32),
            dma((3,)),
            dma((3, NX)),
            dma((NX,)),
            dma((3,)),
            dma((3,)),
            dma((3, NX)),
            dma((NX,)),
            dma((2, 2)),
            dma((2, 2)),
            dma((2, 2, NZ)),
            dma((2, 2, NZ)),
            dma((2,)),
            dma((2,)),
            dma((2, NX)),
            dma((2 * NX,)),
            pltpu.SemaphoreType.REGULAR,
        ],
        compiler_params=pltpu.CompilerParams(
            collective_id=0, has_side_effects=True, vmem_limit_bytes=63 << 20
        ),
        name="project",
    )(image_rows, enc_gain, key_value_w)
    return pl.pallas_call(
        attend,
        out_shape=jax.ShapeDtypeStruct(queries.shape, bf16),
        in_specs=[pl.BlockSpec(memory_space=pltpu.SMEM), vmem, vmem],
        out_specs=vmem,
        compiler_params=pltpu.CompilerParams(vmem_limit_bytes=16 << 20),
        name="attend",
    )(tiles, parts, queries)


def solution(mesh):
    return jax.shard_map(
        shards,
        mesh=mesh,
        in_specs=(
            P(("grp", "fsdp"), "tp"),
            P("tp"),
            P(("tp", "fsdp"), None),
            P("fsdp"),
            P(("grp", "fsdp"), "tp"),
        ),
        out_specs=P(("grp", "fsdp"), "tp"),
        check_vma=False,
    )
```

time: 218 us -> 69.3 us (0.32)
  the two profiles are of different devices: /device:TPU:1 before, /device:TPU:31 now
where the time goes in v2:
time: 69.3 us; the launch traced here: 69.1 us
  Pallas kernels  68 us (98%)
  local copies, waits for them, and re-layouts  1.04 us (2%)
    pallas_call x1, Pallas kernels, shards(): pl.pallas_call(project, out_shape=jax.ShapeDtypeStruct((2 * NX, IMG, 2 *...  65.5 us
    pallas_call x1, Pallas kernels, shards(): pl.pallas_call(attend, out_shape=jax.ShapeDtypeStruct(queries.shape, bf16...  2.51 us

profile of v2, /device:TPU:31, one launch (start us, length us, event | category | flops | bytes accessed | tf_op | source)
XLA Modules:
  0.0 69.1 jit_solution(8212068283523497449)
XLA Ops:
  0.0 0.0 copy-start.1
  0.0 0.0 copy-start.2
  0.0 65.5 %project.1.part_ref = bf16[8,128,256]{2,1,0:T(8,128)(2,1)} custom-call(bf16[384,2048]{1,0:T(8,128)(2,1)} %rows_hbm.1, bf16[2048]{0:T(1024)(128)(2,1)} %gain_hbm.1, bf16[32,1024]{1,0:T(8,128)(2,1)} %w_hbm.1), custom_call_target="tpu_custom_call" | custom-call | tf_op jit(solution)/shard_map/project/pallas_call | solution.py:350
  65.5 0.0 copy-done.1
  65.6 0.0 copy-done.2
  65.6 0.0 copy-start
  65.6 1.0 %copy-done = bf16[8,128,256]{2,1,0:T(8,128)(2,1)S(1)} copy-done((bf16[8,128,256]{2,1,0:T(8,128)(2,1)S(1)}, bf16[8,128,256]{2,1,0:T(8,128)(2,1)}, u32[]{:S(2)}) %copy-start) | copy-done | bytes 524312
  66.6 2.5 %attend.1 = bf16[256,1024]{1,0:T(8,128)(2,1)} custom-call(s32[6]{0:T(128)S(1)} %copy-done.2, bf16[8,128,256]{2,1,0:T(8,128)(2,1)S(1)} %copy-done, bf16[256,1024]{1,0:T(8,128)(2,1)S(1)} %copy-done.1), custom_call_target="tpu_custom_call" | custom-call | tf_op jit(solution)/shard_map/attend/pallas_call | solution.py:389
Async XLA Ops:
  0.0 65.6 %copy-start.1 = (bf16[256,1024]{1,0:T(8,128)(2,1)S(1)}, bf16[256,1024]{1,0:T(8,128)(2,1)}, u32[]{:S(2)}) copy-start(bf16[256,1024]{1,0:T(8,128)(2,1)} %q_ref.1) | copy-start | bytes 1572868
  0.0 65.6 %copy-start.2 = (s32[6]{0:T(128)S(1)}, s32[6]{0:T(128)}, u32[]{:S(2)}) copy-start(s32[6]{0:T(128)} %tiles_ref.1) | copy-start | bytes 76
  65.6 1.0 %copy-start = (bf16[8,128,256]{2,1,0:T(8,128)(2,1)S(1)}, bf16[8,128,256]{2,1,0:T(8,128)(2,1)}, u32[]{:S(2)}) copy-start(bf16[8,128,256]{2,1,0:T(8,128)(2,1)} %project.1.part_ref) | copy-start | bytes 1572868

commit v3 on v2

--- a/solution.py
+++ b/solution.py
@@ -20,14 +20,15 @@
 PIECE = 32
 PART = 512
 SPARE = 2
+TURN = (2, 1, 3, 0)
 MESH = pl.DeviceIdType.MESH
 
 
 def project(
     rows_hbm, gain_hbm, w_hbm, out_ref,
-    rows, gain_ref, inbox, normed, wz, mine, theirs, packed, stat, scale, scale_in,
+    rows, gain_ref, inbox, normed, wz, mine, theirs, kept, packed, parts, half, stat, scale, scale_in,
     local_sem, rows_send, rows_recv, stat_send, stat_recv, scale_send, scale_recv,
-    far_send, far_recv, near_send, near_recv, core_send, core_recv, part_send, part_recv, ready,
+    far_send, far_recv, near_send, near_recv, core_send, core_recv, half_send, half_recv, part_send, part_recv, ready,
 ):
     g = lax.axis_index("grp")
     f = lax.axis_index("fsdp")
@@ -62,7 +63,7 @@
 
     @pl.when(g == SPARE)
     def _():
-        pl.semaphore_wait(barrier, 8)
+        pl.semaphore_wait(barrier, 4)
 
     @pl.when(g != SPARE)
     def _():
@@ -84,8 +85,7 @@
                 for xd in range(NX):
                     hello(chip(gg, xs(xd), z, t))
             for xd in range(NX):
-                for yy in (0, 1):
-                    hello(chip(SPARE, xs(xd), z, yy * 2 + core))
+                hello(chip(SPARE, xs(xd), z, (1 - ylo) * 2 + core))
 
         @pl.when(g > 0)
         def _():
@@ -148,7 +148,7 @@
 
         @pl.when(g == 0)
         def _():
-            for xd in range(NX):
+            for xd in TURN:
                 for i, (gg, block) in enumerate(targets):
                     if gg == 0 and xd == 0:
                         own_inbox().start()
@@ -222,70 +222,101 @@
             for i in (1, 2, 3):
                 pick = jnp.where(x == i, gain_ref[i * PART + j * 128:i * PART + (j + 1) * 128], pick)
             gains.append(pick.astype(jnp.float32).reshape(1, 128))
-        for i in range(NX):
-            got(inbox.at[i], rows_recv.at[i])
-            got(scale_in.at[i], scale_recv.at[i])
-            column = jnp.transpose(jnp.broadcast_to(scale_in[i, 0:1], (128, IMG)))
-            for j in range(PART // 128):
-                lanes = slice(j * 128, (j + 1) * 128)
-                normed[i * IMG:(i + 1) * IMG, lanes] = (
-                    inbox[i, :, lanes].astype(jnp.float32) * column * gains[j]
-                ).astype(jnp.bfloat16)
-
         for c in (0, 1):
             for d in (0, 1):
                 got_near(-3 * way(d), d, c)
                 got_near(-8 * way(d), d, c)
                 got_near(4 * way(d), d, c)
 
-        def head(h):
-            w = wz[:, :, pl.ds(pl.multiple_of(h * 256, 256), 256)].reshape(PART, 256)
-            return jnp.dot(normed[...], w, preferred_element_type=jnp.float32)
+        slot = x * 2 + ylo
 
         def side(j):
             return ylo if j == 0 else 1 - ylo
 
-        order = (1, 0)
-        for j in order:
-            mine[j] = head(side(j) * 2 + 1 - core)
-            push(mine.at[j], theirs.at[j], core_send.at[j], core_recv.at[j], (g, f, ylo * 2 + 1 - core))
-
-        home = jnp.where(g == 0, SPARE, g)
-        slot = x * 2 + ylo
-
-        @pl.when(g == 0)
-        def _():
-            pl.semaphore_wait(ready, 8)
-
-        def own_part():
+        def head(i, h):
+            w = wz[:, :, pl.ds(pl.multiple_of(h * 256, 256), 256)].reshape(PART, 256)
+            return jnp.dot(normed[i], w, preferred_element_type=jnp.float32)
+
+        partner = (0, f, (1 - ylo) * 2 + core)
+
+        def across(i):
+            return copy(packed.at[i, 0], half.at[i], half_send.at[i], half_recv.at[i], partner)
+
+        def part_copy(i, j, xd):
+            gg = SPARE if j == 2 else g
             return copy(
-                packed.at[0, pl.ds(pl.multiple_of(x * IMG, IMG), IMG)], out_ref.at[slot],
-                part_send.at[0, 0], part_recv.at[slot], chip(SPARE, x, z, t),
+                packed.at[i, min(j, 1)], parts.at[slot], part_send.at[min(j, 1), xd], part_recv.at[slot],
+                chip(gg, xs(-xd), z, side(min(j, 1)) * 2 + core),
             )
 
-        for j in order:
-            own = head(side(j) * 2 + core)
-            got(theirs.at[j], core_recv.at[j])
-            packed[j] = (own + theirs[j]).astype(jnp.bfloat16)
-            for xd in (2, 1, 3, 0):
-                src = packed.at[j, pl.ds(pl.multiple_of(xs(xd) * IMG, IMG), IMG)]
-                if j == 0 and xd == 0:
-                    @pl.when(g == 0)
-                    def _():
-                        own_part().start()
-
-                    @pl.when(g > 0)
-                    def _():
-                        pltpu.make_async_copy(src, out_ref.at[slot], part_recv.at[slot]).start()
-                else:
-                    push(
-                        src, out_ref.at[slot], part_send.at[j, xd], part_recv.at[slot],
-                        chip(home, xs(xd), z, side(j) * 2 + core),
-                    )
-
-        @pl.when(g == 0)
-        def _():
-            own_part().wait_send()
+        def begin(i, xd):
+            src = xs(-xd)
+            got(inbox.at[src], rows_recv.at[src])
+            if i == 0:
+                for k in range(NX):
+                    got(scale_in.at[k], scale_recv.at[k])
+            column = jnp.transpose(jnp.broadcast_to(scale_in[src, 0:1], (128, IMG)))
+            for j in range(PART // 128):
+                lanes = slice(j * 128, (j + 1) * 128)
+                normed[i, :, lanes] = (
+                    inbox[src, :, lanes].astype(jnp.float32) * column * gains[j]
+                ).astype(jnp.bfloat16)
+            for j in (0, 1):
+                mine[i, j] = head(i, side(j) * 2 + 1 - core)
+            push(mine.at[i], theirs.at[i], core_send.at[i], core_recv.at[i], (g, f, ylo * 2 + 1 - core))
+            for j in (0, 1):
+                kept[i, j] = head(i, side(j) * 2 + core)
+
+        def finish(i, xd):
+            got(theirs.at[i], core_recv.at[i])
+
+            @pl.when(g == 0)
+            def _():
+                packed[i, 0] = (kept[i, 0] + theirs[i, 0]).astype(jnp.bfloat16)
+                across(i).start()
+
+            @pl.when(g > 0)
+            def _():
+                for j in (1, 0):
+                    packed[i, j] = (kept[i, j] + theirs[i, j]).astype(jnp.bfloat16)
+                    if j == 0 and xd == 0:
+                        pltpu.make_async_copy(packed.at[i, j], parts.at[slot], part_recv.at[slot]).start()
+                    else:
+                        part_copy(i, j, xd).start()
+
+        def final(i, xd):
+            @pl.when(g == 0)
+            def _():
+                if i == 0:
+                    pl.semaphore_wait(ready, 4)
+                got(half.at[i], half_recv.at[i])
+                packed[i, 1] = (
+                    (kept[i, 1] + theirs[i, 1]) + half[i].astype(jnp.float32)
+                ).astype(jnp.bfloat16)
+                part_copy(i, 2, xd).start()
+
+        for i in range(NX):
+            begin(i, TURN[i])
+            if i >= 1:
+                finish(i - 1, TURN[i - 1])
+            if i >= 2:
+                final(i - 2, TURN[i - 2])
+        finish(NX - 1, TURN[NX - 1])
+        final(NX - 2, TURN[NX - 2])
+        final(NX - 1, TURN[NX - 1])
+
+        @pl.when(g > 0)
+        def _():
+            for i, xd in enumerate(TURN):
+                for j in (1, 0):
+                    if j == 1 or xd != 0:
+                        part_copy(i, j, xd).wait_send()
+
+        @pl.when(g == 0)
+        def _():
+            for i, xd in enumerate(TURN):
+                across(i).wait_send()
+                part_copy(i, 2, xd).wait_send()
             for d in (1, 2, 3):
                 stat_copy(d).wait_send()
             for xd in range(NX):
@@ -300,34 +331,39 @@
     @pl.when(g == SPARE)
     def _():
         for xd in range(NX):
-            for yy in (0, 1):
-                pl.semaphore_signal(
-                    ready, inc=1, device_id=chip(0, xs(xd), z, yy * 2 + core), device_id_type=MESH
-                )
+            pl.semaphore_signal(
+                ready, inc=1, device_id=chip(0, xs(xd), z, (1 - ylo) * 2 + core), device_id_type=MESH
+            )
+
+    def gather_parts(slots):
+        total = jnp.zeros((IMG, 2 * HD), jnp.float32)
+        for i in slots:
+            got(parts.at[i], part_recv.at[i])
+            total = total + parts[i].astype(jnp.float32)
+        out_ref[...] = total.astype(jnp.bfloat16)
+
+    @pl.when(g == SPARE)
+    def _():
+        gather_parts([xs(-xd) * 2 + 1 - ylo for xd in TURN])
+
+    @pl.when((g > 0) & (g != SPARE))
+    def _():
+        gather_parts(range(2 * NX))
+
+
+def attend(tiles_ref, kv_ref, q_ref, o_ref):
+    g = lax.axis_index("grp")
+
+    @pl.when(g == 0)
+    def _():
+        o_ref[...] = jnp.zeros_like(o_ref)
 
     @pl.when(g > 0)
     def _():
-        for i in range(2 * NX):
-            got(out_ref.at[i], part_recv.at[i])
-
-
-def attend(tiles_ref, part_ref, q_ref, o_ref):
-    g = lax.axis_index("grp")
-
-    @pl.when(g == 0)
-    def _():
-        o_ref[...] = jnp.zeros_like(o_ref)
-
-    @pl.when(g > 0)
-    def _():
-        kv = part_ref[0].astype(jnp.float32)
-        for i in range(1, 2 * NX):
-            kv = kv + part_ref[i].astype(jnp.float32)
-        kv = kv.astype(jnp.bfloat16)
         slot = lax.broadcasted_iota(jnp.int32, (TXT_S, CAP), 1)
         for s in range(SAMP):
-            keys = kv[s * CAP:(s + 1) * CAP, :HD]
-            values = kv[s * CAP:(s + 1) * CAP, HD:]
+            keys = kv_ref[s * CAP:(s + 1) * CAP, :HD]
+            values = kv_ref[s * CAP:(s + 1) * CAP, HD:]
             live = slot < tiles_ref[(g - 1) * SAMP + s] * TILE_TOK
             for h in range(QH // KVH):
                 q = q_ref[s * TXT_S:(s + 1) * TXT_S, h * HD:(h + 1) * HD]
@@ -347,20 +383,23 @@
     bf16, f32 = jnp.bfloat16, jnp.float32
     hbm = pl.BlockSpec(memory_space=pltpu.HBM)
     vmem = pl.BlockSpec(memory_space=pltpu.VMEM)
-    parts = pl.pallas_call(
+    kv = pl.pallas_call(
         project,
-        out_shape=jax.ShapeDtypeStruct((2 * NX, IMG, 2 * HD), bf16),
+        out_shape=jax.ShapeDtypeStruct((IMG, 2 * HD), bf16),
         in_specs=[hbm, hbm, hbm],
-        out_specs=hbm,
+        out_specs=vmem,
         scratch_shapes=[
             pltpu.VMEM((3 * IMG, 2048), bf16),
             pltpu.VMEM((2048,), bf16),
             pltpu.VMEM((NX, IMG, PART), bf16),
-            pltpu.VMEM((NX * IMG, PART), bf16),
+            pltpu.VMEM((NX, IMG, PART), bf16),
             pltpu.VMEM((NZ, PIECE, 1024), bf16),
-            pltpu.VMEM((2, NX * IMG, 256), f32),
-            pltpu.VMEM((2, NX * IMG, 256), f32),
-            pltpu.VMEM((2, NX * IMG, 256), bf16),
+            pltpu.VMEM((NX, 2, IMG, 256), f32),
+            pltpu.VMEM((NX, 2, IMG, 256), f32),
+            pltpu.VMEM((NX, 2, IMG, 256), f32),
+            pltpu.VMEM((NX, 2, IMG, 256), bf16),
+            pltpu.VMEM((2 * NX, IMG, 256), bf16),
+            pltpu.VMEM((NX, IMG, 256), bf16),
             pltpu.VMEM((4, 8, 3 * IMG), f32),
             pltpu.VMEM((3, 8, IMG), f32),
             pltpu.VMEM((NX, 8, IMG), f32),
@@ -375,8 +414,10 @@
             dma((2, 2)),
             dma((2, 2, NZ)),
             dma((2, 2, NZ)),
-            dma((2,)),
-            dma((2,)),
+            dma((NX,)),
+            dma((NX,)),
+            dma((NX,)),
+            dma((NX,)),
             dma((2, NX)),
             dma((2 * NX,)),
             pltpu.SemaphoreType.REGULAR,
@@ -393,7 +434,7 @@
         out_specs=vmem,
         compiler_params=pltpu.CompilerParams(vmem_limit_bytes=16 << 20),
         name="attend",
-    )(tiles, parts, queries)
+    )(tiles, kv, queries)
 
 
 def solution(mesh):

time: 69.3 us -> 64.4 us (0.929)
  the two profiles are of different devices: /device:TPU:31 before, /device:TPU:1 now
where the time goes in v3:
time: 64.4 us; the launch traced here: 63.2 us
  Pallas kernels  62.3 us (97%)
  local copies, waits for them, and re-layouts  0.84 us (1%)
    pallas_call x1, Pallas kernels, shards(): pl.pallas_call(project, out_shape=jax.ShapeDtypeStruct((IMG, 2 * HD), bf1...  60.9 us
    pallas_call x1, Pallas kernels, shards(): pl.pallas_call(attend, out_shape=jax.ShapeDtypeStruct(queries.shape, bf16...  1.38 us

profile of v3, /device:TPU:1, one launch (start us, length us, event | category | flops | bytes accessed | tf_op | source)
XLA Modules:
  0.0 63.2 jit_solution(6579738881662270022)
XLA Ops:
  0.0 0.0 copy-start
  0.0 0.0 copy-start.2
  0.0 60.9 %project.1.kv_ref = bf16[128,256]{1,0:T(8,128)(2,1)} custom-call(bf16[384,2048]{1,0:T(8,128)(2,1)} %rows_hbm.1, bf16[2048]{0:T(1024)(128)(2,1)} %gain_hbm.1, bf16[32,1024]{1,0:T(8,128)(2,1)} %w_hbm.1), custom_call_target="tpu_custom_call" | custom-call | tf_op jit(solution)/shard_map/project/pallas_call | solution.py:386
  60.9 0.0 copy-done
  60.9 0.0 copy-done.2
  60.9 0.0 copy-start.1
  60.9 0.8 %copy-done.1 = bf16[128,256]{1,0:T(8,128)(2,1)S(1)} copy-done((bf16[128,256]{1,0:T(8,128)(2,1)S(1)}, bf16[128,256]{1,0:T(8,128)(2,1)}, u32[]{:S(2)}) %copy-start.1) | copy-done | bytes 65560
  61.8 1.4 %attend.1 = bf16[256,1024]{1,0:T(8,128)(2,1)} custom-call(s32[6]{0:T(128)S(1)} %copy-done.2, bf16[128,256]{1,0:T(8,128)(2,1)S(1)} %copy-done.1, bf16[256,1024]{1,0:T(8,128)(2,1)S(1)} %copy-done), custom_call_target="tpu_custom_call" | custom-call | tf_op jit(solution)/shard_map/attend/pallas_call | solution.py:430
Async XLA Ops:
  0.0 60.9 %copy-start = (bf16[256,1024]{1,0:T(8,128)(2,1)S(1)}, bf16[256,1024]{1,0:T(8,128)(2,1)}, u32[]{:S(2)}) copy-start(bf16[256,1024]{1,0:T(8,128)(2,1)} %q_ref.1) | copy-start | bytes 1572868
  0.0 60.9 %copy-start.2 = (s32[6]{0:T(128)S(1)}, s32[6]{0:T(128)}, u32[]{:S(2)}) copy-start(s32[6]{0:T(128)} %tiles_ref.1) | copy-start | bytes 76
  60.9 0.8 %copy-start.1 = (bf16[128,256]{1,0:T(8,128)(2,1)S(1)}, bf16[128,256]{1,0:T(8,128)(2,1)}, u32[]{:S(2)}) copy-start(bf16[128,256]{1,0:T(8,128)(2,1)} %project.1.kv_ref) | copy-start | bytes 196612

commit v4 on v3

--- a/solution.py
+++ b/solution.py
@@ -148,12 +148,12 @@
 
         @pl.when(g == 0)
         def _():
+            own_inbox().start()
+            for xd in TURN[:3]:
+                rows_copy(2, 0, 1, xd).start()
             for xd in TURN:
-                for i, (gg, block) in enumerate(targets):
-                    if gg == 0 and xd == 0:
-                        own_inbox().start()
-                    else:
-                        rows_copy(i, gg, block, xd).start()
+                for i, (gg, block) in enumerate(targets[:2]):
+                    rows_copy(i, gg, block, xd).start()
 
         for c in (0, 1):
             for d in (0, 1):
@@ -201,14 +201,14 @@
 
         for c in (0, 1):
             for d in (0, 1):
+                got(wz.at[zs(-FAR * way(d)), :, cols(c)], far_recv.at[d, c])
+            for d in (0, 1):
+                near(-FAR * way(d), d, c)
+                near(FAR * way(d), d, c)
+        for c in (0, 1):
+            for d in (0, 1):
                 got_near(-2 * way(d), d, c)
                 near(-2 * way(d), d, c)
-        for c in (0, 1):
-            for d in (0, 1):
-                got(wz.at[zs(-FAR * way(d)), :, cols(c)], far_recv.at[d, c])
-            for d in (0, 1):
-                near(-FAR * way(d), d, c)
-                near(FAR * way(d), d, c)
         for c in (0, 1):
             for d in (0, 1):
                 got_near(-7 * way(d), d, c)

time: 64.4 us -> 63.6 us (0.988)
  Pallas kernels: 62.3 us -> 61.5 us
    pallas_call x1, Pallas kernels: 60.9 us -> 60.1 us  [shards(): pl.pallas_call(project, out_shape=jax.ShapeDtypeStruct((IMG, 2 * HD), bf1...]
where the time goes in v4:
time: 63.6 us; the launch traced here: 62.3 us
  Pallas kernels  61.5 us (97%)
  local copies, waits for them, and re-layouts  0.84 us (1%)
    pallas_call x1, Pallas kernels, shards(): pl.pallas_call(project, out_shape=jax.ShapeDtypeStruct((IMG, 2 * HD), bf1...  60.1 us
    pallas_call x1, Pallas kernels, shards(): pl.pallas_call(attend, out_shape=jax.ShapeDtypeStruct(queries.shape, bf16...  1.38 us

profile of v4, /device:TPU:1, one launch (start us, length us, event | category | flops | bytes accessed | tf_op | source)
XLA Modules:
  0.0 62.3 jit_solution(766941077117180285)
XLA Ops:
  0.0 0.0 copy-start
  0.0 0.0 copy-start.2
  0.0 60.1 %project.1.kv_ref = bf16[128,256]{1,0:T(8,128)(2,1)} custom-call(bf16[384,2048]{1,0:T(8,128)(2,1)} %rows_hbm.1, bf16[2048]{0:T(1024)(128)(2,1)} %gain_hbm.1, bf16[32,1024]{1,0:T(8,128)(2,1)} %w_hbm.1), custom_call_target="tpu_custom_call" | custom-call | tf_op jit(solution)/shard_map/project/pallas_call | solution.py:386
  60.1 0.0 copy-done
  60.1 0.0 copy-done.2
  60.1 0.0 copy-start.1
  60.1 0.8 %copy-done.1 = bf16[128,256]{1,0:T(8,128)(2,1)S(1)} copy-done((bf16[128,256]{1,0:T(8,128)(2,1)S(1)}, bf16[128,256]{1,0:T(8,128)(2,1)}, u32[]{:S(2)}) %copy-start.1) | copy-done | bytes 65560
  61.0 1.4 %attend.1 = bf16[256,1024]{1,0:T(8,128)(2,1)} custom-call(s32[6]{0:T(128)S(1)} %copy-done.2, bf16[128,256]{1,0:T(8,128)(2,1)S(1)} %copy-done.1, bf16[256,1024]{1,0:T(8,128)(2,1)S(1)} %copy-done), custom_call_target="tpu_custom_call" | custom-call | tf_op jit(solution)/shard_map/attend/pallas_call | solution.py:430
Async XLA Ops:
  0.0 60.1 %copy-start = (bf16[256,1024]{1,0:T(8,128)(2,1)S(1)}, bf16[256,1024]{1,0:T(8,128)(2,1)}, u32[]{:S(2)}) copy-start(bf16[256,1024]{1,0:T(8,128)(2,1)} %q_ref.1) | copy-start | bytes 1572868
  0.0 60.1 %copy-start.2 = (s32[6]{0:T(128)S(1)}, s32[6]{0:T(128)}, u32[]{:S(2)}) copy-start(s32[6]{0:T(128)} %tiles_ref.1) | copy-start | bytes 76
  60.1 0.8 %copy-start.1 = (bf16[128,256]{1,0:T(8,128)(2,1)S(1)}, bf16[128,256]{1,0:T(8,128)(2,1)}, u32[]{:S(2)}) copy-start(bf16[128,256]{1,0:T(8,128)(2,1)} %project.1.kv_ref) | copy-start | bytes 196612

commit v5 on v4

--- a/solution.py
+++ b/solution.py
@@ -162,6 +162,11 @@
         def stat_copy(d):
             return copy(stat.at[0], stat.at[d], stat_send.at[d - 1], stat_recv.at[d - 1], (0, f, (t + d) % 4))
 
+        for c in (0, 1):
+            for d in (0, 1):
+                got_near(-way(d), d, c)
+                near(-way(d), d, c)
+
         @pl.when(g == 0)
         def _():
             own_rows.wait()
@@ -174,16 +179,17 @@
             for d in (1, 2, 3):
                 stat_copy(d).start()
 
-        for c in (0, 1):
-            for d in (0, 1):
-                got_near(-way(d), d, c)
-                near(-way(d), d, c)
-
         def scale_copy(i, gg, block, xd):
             return copy(
                 scale.at[block], scale_in.at[x], scale_send.at[i, xd], scale_recv.at[x], chip(gg, xs(xd), z, t)
             )
 
+        for c in (0, 1):
+            for d in (0, 1):
+                got(wz.at[zs(-FAR * way(d)), :, cols(c)], far_recv.at[d, c])
+            for d in (0, 1):
+                near(-FAR * way(d), d, c)
+                near(FAR * way(d), d, c)
         @pl.when(g == 0)
         def _():
             for d in (1, 2, 3):
@@ -199,12 +205,6 @@
                     else:
                         scale_copy(i, gg, block, xd).start()
 
-        for c in (0, 1):
-            for d in (0, 1):
-                got(wz.at[zs(-FAR * way(d)), :, cols(c)], far_recv.at[d, c])
-            for d in (0, 1):
-                near(-FAR * way(d), d, c)
-                near(FAR * way(d), d, c)
         for c in (0, 1):
             for d in (0, 1):
                 got_near(-2 * way(d), d, c)

time: 63.6 us -> 61.7 us (0.970)
  the two profiles are of different devices: /device:TPU:1 before, /device:TPU:53 now
where the time goes in v5:
time: 61.7 us; the launch traced here: 61.5 us
  Pallas kernels  60.6 us (98%)
  local copies, waits for them, and re-layouts  0.84 us (1%)
    pallas_call x1, Pallas kernels, shards(): pl.pallas_call(project, out_shape=jax.ShapeDtypeStruct((IMG, 2 * HD), bf1...  58.1 us
    pallas_call x1, Pallas kernels, shards(): pl.pallas_call(attend, out_shape=jax.ShapeDtypeStruct(queries.shape, bf16...  2.5 us

profile of v5, /device:TPU:53, one launch (start us, length us, event | category | flops | bytes accessed | tf_op | source)
XLA Modules:
  0.0 61.5 jit_solution(17026414154496604673)
XLA Ops:
  0.0 0.0 copy-start
  0.0 0.0 copy-start.2
  0.0 58.1 %project.1.kv_ref = bf16[128,256]{1,0:T(8,128)(2,1)} custom-call(bf16[384,2048]{1,0:T(8,128)(2,1)} %rows_hbm.1, bf16[2048]{0:T(1024)(128)(2,1)} %gain_hbm.1, bf16[32,1024]{1,0:T(8,128)(2,1)} %w_hbm.1), custom_call_target="tpu_custom_call" | custom-call | tf_op jit(solution)/shard_map/project/pallas_call | solution.py:386
  58.1 0.0 copy-done
  58.1 0.0 copy-done.2
  58.1 0.0 copy-start.1
  58.1 0.8 %copy-done.1 = bf16[128,256]{1,0:T(8,128)(2,1)S(1)} copy-done((bf16[128,256]{1,0:T(8,128)(2,1)S(1)}, bf16[128,256]{1,0:T(8,128)(2,1)}, u32[]{:S(2)}) %copy-start.1) | copy-done | bytes 65560
  59.0 2.5 %attend.1 = bf16[256,1024]{1,0:T(8,128)(2,1)} custom-call(s32[6]{0:T(128)S(1)} %copy-done.2, bf16[128,256]{1,0:T(8,128)(2,1)S(1)} %copy-done.1, bf16[256,1024]{1,0:T(8,128)(2,1)S(1)} %copy-done), custom_call_target="tpu_custom_call" | custom-call | tf_op jit(solution)/shard_map/attend/pallas_call | solution.py:430
Async XLA Ops:
  0.0 58.1 %copy-start = (bf16[256,1024]{1,0:T(8,128)(2,1)S(1)}, bf16[256,1024]{1,0:T(8,128)(2,1)}, u32[]{:S(2)}) copy-start(bf16[256,1024]{1,0:T(8,128)(2,1)} %q_ref.1) | copy-start | bytes 1572868
  0.0 58.1 %copy-start.2 = (s32[6]{0:T(128)S(1)}, s32[6]{0:T(128)}, u32[]{:S(2)}) copy-start(s32[6]{0:T(128)} %tiles_ref.1) | copy-start | bytes 76
  58.1 0.8 %copy-start.1 = (bf16[128,256]{1,0:T(8,128)(2,1)S(1)}, bf16[128,256]{1,0:T(8,128)(2,1)}, u32[]{:S(2)}) copy-start(bf16[128,256]{1,0:T(8,128)(2,1)} %project.1.kv_ref) | copy-start | bytes 196612

commit v6 on v5

--- a/solution.py
+++ b/solution.py
@@ -167,6 +167,17 @@
                 got_near(-way(d), d, c)
                 near(-way(d), d, c)
 
+        def scale_copy(i, gg, block, xd):
+            return copy(
+                scale.at[block], scale_in.at[x], scale_send.at[i, xd], scale_recv.at[x], chip(gg, xs(xd), z, t)
+            )
+
+        for c in (0, 1):
+            for d in (0, 1):
+                got(wz.at[zs(-FAR * way(d)), :, cols(c)], far_recv.at[d, c])
+            for d in (0, 1):
+                near(-FAR * way(d), d, c)
+                near(FAR * way(d), d, c)
         @pl.when(g == 0)
         def _():
             own_rows.wait()
@@ -179,17 +190,10 @@
             for d in (1, 2, 3):
                 stat_copy(d).start()
 
-        def scale_copy(i, gg, block, xd):
-            return copy(
-                scale.at[block], scale_in.at[x], scale_send.at[i, xd], scale_recv.at[x], chip(gg, xs(xd), z, t)
-            )
-
-        for c in (0, 1):
-            for d in (0, 1):
-                got(wz.at[zs(-FAR * way(d)), :, cols(c)], far_recv.at[d, c])
-            for d in (0, 1):
-                near(-FAR * way(d), d, c)
-                near(FAR * way(d), d, c)
+        for c in (0, 1):
+            for d in (0, 1):
+                got_near(-2 * way(d), d, c)
+                near(-2 * way(d), d, c)
         @pl.when(g == 0)
         def _():
             for d in (1, 2, 3):
@@ -205,10 +209,6 @@
                     else:
                         scale_copy(i, gg, block, xd).start()
 
-        for c in (0, 1):
-            for d in (0, 1):
-                got_near(-2 * way(d), d, c)
-                near(-2 * way(d), d, c)
         for c in (0, 1):
             for d in (0, 1):
                 got_near(-7 * way(d), d, c)

time: 61.7 us -> 62 us (level)
  the two profiles are of different devices: /device:TPU:53 before, /device:TPU:1 now
where the time goes in v6:
time: 62 us; the launch traced here: 60.8 us
  Pallas kernels  59.9 us (97%)
  local copies, waits for them, and re-layouts  0.84 us (1%)
    pallas_call x1, Pallas kernels, shards(): pl.pallas_call(project, out_shape=jax.ShapeDtypeStruct((IMG, 2 * HD), bf1...  58.5 us
    pallas_call x1, Pallas kernels, shards(): pl.pallas_call(attend, out_shape=jax.ShapeDtypeStruct(queries.shape, bf16...  1.38 us

profile of v6, /device:TPU:1, one launch (start us, length us, event | category | flops | bytes accessed | tf_op | source)
XLA Modules:
  0.0 60.8 jit_solution(6118688603961397917)
XLA Ops:
  0.0 0.0 copy-start
  0.0 0.0 copy-start.2
  0.0 58.5 %project.1.kv_ref = bf16[128,256]{1,0:T(8,128)(2,1)} custom-call(bf16[384,2048]{1,0:T(8,128)(2,1)} %rows_hbm.1, bf16[2048]{0:T(1024)(128)(2,1)} %gain_hbm.1, bf16[32,1024]{1,0:T(8,128)(2,1)} %w_hbm.1), custom_call_target="tpu_custom_call" | custom-call | tf_op jit(solution)/shard_map/project/pallas_call | solution.py:386
  58.5 0.0 copy-done
  58.6 0.0 copy-done.2
  58.6 0.0 copy-start.1
  58.6 0.8 %copy-done.1 = bf16[128,256]{1,0:T(8,128)(2,1)S(1)} copy-done((bf16[128,256]{1,0:T(8,128)(2,1)S(1)}, bf16[128,256]{1,0:T(8,128)(2,1)}, u32[]{:S(2)}) %copy-start.1) | copy-done | bytes 65560
  59.4 1.4 %attend.1 = bf16[256,1024]{1,0:T(8,128)(2,1)} custom-call(s32[6]{0:T(128)S(1)} %copy-done.2, bf16[128,256]{1,0:T(8,128)(2,1)S(1)} %copy-done.1, bf16[256,1024]{1,0:T(8,128)(2,1)S(1)} %copy-done), custom_call_target="tpu_custom_call" | custom-call | tf_op jit(solution)/shard_map/attend/pallas_call | solution.py:430
Async XLA Ops:
  0.0 58.5 %copy-start = (bf16[256,1024]{1,0:T(8,128)(2,1)S(1)}, bf16[256,1024]{1,0:T(8,128)(2,1)}, u32[]{:S(2)}) copy-start(bf16[256,1024]{1,0:T(8,128)(2,1)} %q_ref.1) | copy-start | bytes 1572868
  0.0 58.6 %copy-start.2 = (s32[6]{0:T(128)S(1)}, s32[6]{0:T(128)}, u32[]{:S(2)}) copy-start(s32[6]{0:T(128)} %tiles_ref.1) | copy-start | bytes 76
  58.6 0.8 %copy-start.1 = (bf16[128,256]{1,0:T(8,128)(2,1)S(1)}, bf16[128,256]{1,0:T(8,128)(2,1)}, u32[]{:S(2)}) copy-start(bf16[128,256]{1,0:T(8,128)(2,1)} %project.1.kv_ref) | copy-start | bytes 196612
